TPU v7x, 32 devices: a whole 2x2x4 slice. The times are simulated.
32 devices in a mesh: lon: 2 (over x), lat: 4 (over z), tm: 4 (over y, core).
Axes of the slice: x: 2, y: 2, z: 4, core: 2. Of those that a mesh axis runs over, the one named last changes fastest.
Arguments:
- precip: float32 [128, 1024, 256], P('tm', 'lat', 'lon'), may hold values from 0.02 to 8
- offset: float32 [128, 1024, 256], P('tm', 'lat', 'lon'), may hold values from -3 to 3
- coefficients: float32 [32, 256, 64], P('tm', 'lat', 'lon'), may hold values from -2 to 2
- inverse_diag: float32 [32, 256, 64], P('tm', 'lat', 'lon'), may hold values from 0.02 to 0.2
Outputs:
- newton_step: float32 [32, 256, 64], P('tm', 'lat', 'lon')
- residual: float32 [32, 256, 64], P('tm', 'lat', 'lon')
All inputs are finite; a program needn't handle non-finite values.
Results may differ from a plain program's by a relative error of at most 0.0003.
Values sent between devices are 32-bit elements; how exact they have to be, the bound alone decides.
A program may use at most 64 MiB of HBM per device.

v0:
```python
import jax
import jax.numpy as jnp
from jax import lax
from jax.sharding import PartitionSpec as P

tweedie_power = 1.6
smooth = 0.5
highest = lax.Precision.HIGHEST


def with_halo(cells, sides, width, closed):
    for axis, dim in sides:
        count = lax.axis_size(axis)
        ends = count if closed else count - 1
        head = lax.slice_in_dim(cells, 0, width, axis=dim)
        tail = lax.slice_in_dim(cells, cells.shape[dim] - width, cells.shape[dim], axis=dim)
        cells = jnp.concatenate(
            [
                lax.ppermute(tail, axis, [(i, (i + 1) % count) for i in range(ends)]),
                cells,
                lax.ppermute(head, axis, [((i + 1) % count, i) for i in range(ends)]),
            ],
            axis=dim,
        )
    return cells


def spline(offsets):
    distance = jnp.abs(offsets)
    near_part = (4.0 - 6.0 * distance * distance + 3.0 * distance * distance * distance) / 6.0
    far_part = jnp.maximum(2.0 - distance, 0.0) ** 3 / 6.0
    return jnp.where(distance < 1.0, near_part, far_part)


def synth_table(cell_count, knot_count):
    cell_pos = jnp.arange(cell_count, dtype=jnp.float32)[:, None]
    knot_pos = jnp.arange(knot_count + 4, dtype=jnp.float32)[None, :] - 2.0
    return spline((cell_pos - 4.0 * knot_pos - 1.5) / 4.0)


def expand(values):
    wider = with_halo(values, (("lon", 2),), 2, True)
    return with_halo(wider, (("lat", 1), ("tm", 0)), 2, False)


def evaluate(padded, tables):
    time_tab, lat_tab, lon_tab = tables
    partial_value = jnp.einsum("tae,le->tal", padded, lon_tab, precision=highest)
    partial_value = jnp.einsum("tal,ba->tbl", partial_value, lat_tab, precision=highest)
    return jnp.einsum("tbl,st->sbl", partial_value, time_tab, precision=highest)


def fold_rims(stacked, along, length):
    middle = lax.slice_in_dim(stacked, 4, length + 4, axis=along)
    low_rim = lax.slice_in_dim(stacked, 0, 2, axis=along)
    high_rim = lax.slice_in_dim(stacked, length + 6, length + 8, axis=along)
    filler_shape = list(low_rim.shape)
    filler_shape[along] = length - 2
    filler = jnp.zeros(filler_shape, stacked.dtype)
    return (
        middle
        + jnp.concatenate([low_rim, filler], axis=along)
        + jnp.concatenate([filler, high_rim], axis=along)
    )


def adjoint(cell_values, near_tabs, counts):
    time_count, lat_count, lon_count = counts
    time_tab, lat_tab, lon_tab = near_tabs
    partial_value = jnp.einsum("sbl,st->tbl", cell_values, time_tab, precision=highest)
    partial_value = jnp.einsum("tbl,ba->tal", partial_value, lat_tab, precision=highest)
    partial_value = jnp.einsum("tal,le->tae", partial_value, lon_tab, precision=highest)
    wider = with_halo(partial_value, (("lon", 2),), 2, True)
    wider = fold_rims(wider, 2, lon_count)
    padded = with_halo(wider, (("lat", 1), ("tm", 0)), 2, False)
    return fold_rims(fold_rims(padded, 1, lat_count), 0, time_count)


def penalty(padded, counts):
    time_count, lat_count, lon_count = counts

    def window(time_at, lat_at, lon_at):
        return padded[
            time_at : time_at + time_count, lat_at : lat_at + lat_count, lon_at : lon_at + lon_count
        ]

    summed = 18.0 * window(2, 2, 2)
    for shift_by, factor in ((0, 1.0), (1, -4.0), (3, -4.0), (4, 1.0)):
        summed = summed + factor * (
            window(shift_by, 2, 2) + window(2, shift_by, 2) + window(2, 2, shift_by)
        )
    return smooth * summed


def global_sum(values):
    return lax.psum(values, ("lon", "lat", "tm"))


def per_device(precip, offset, coefficients, inverse_diag):
    time_count, lat_count, lon_count = coefficients.shape
    hour_cells, lat_cells, lon_cells = precip.shape
    counts = (time_count, lat_count, lon_count)
    near_tabs = (
        synth_table(hour_cells, time_count),
        synth_table(lat_cells, lat_count),
        synth_table(lon_cells, lon_count),
    )
    lat_total = lat_cells * lax.axis_size("lat")
    lat_index = (lax.axis_index("lat") * lat_cells + jnp.arange(lat_cells, dtype=jnp.int32)).astype(
        jnp.float32
    )
    area_weight = jnp.cos((90.0 - (lat_index + 0.5) * 180.0 / lat_total) * (jnp.pi / 180.0))[
        None, :, None
    ]
    padded = expand(coefficients)
    linear = offset + evaluate(padded, near_tabs)
    tilted = jnp.exp((1.0 - tweedie_power) * linear)
    mean_rate = jnp.exp(linear)
    weight = area_weight * mean_rate * tilted
    gradient = adjoint(area_weight * (mean_rate - precip) * tilted, near_tabs, counts) + penalty(
        padded, counts
    )
    residual = -gradient
    scaled = inverse_diag * residual
    direction = scaled
    precond_norm = global_sum(jnp.sum(residual * scaled))
    newton_step = jnp.zeros_like(coefficients)
    for sweep in range(2):
        padded_vec = expand(direction)
        image = adjoint(weight * evaluate(padded_vec, near_tabs), near_tabs, counts) + penalty(
            padded_vec, counts
        )
        step_size = precond_norm / global_sum(jnp.sum(direction * image))
        newton_step = newton_step + step_size * direction
        residual = residual - step_size * image
        if sweep == 0:
            scaled = inverse_diag * residual
            next_norm = global_sum(jnp.sum(residual * scaled))
            direction = scaled + next_norm / precond_norm * direction
            precond_norm = next_norm
    return (newton_step, residual)


def solution(mesh):
    return jax.shard_map(
        per_device,
        mesh=mesh,
        in_specs=(
            P("tm", "lat", "lon"),
            P("tm", "lat", "lon"),
            P("tm", "lat", "lon"),
            P("tm", "lat", "lon"),
        ),
        out_specs=(P("tm", "lat", "lon"), P("tm", "lat", "lon")),
        check_vma=False,
    )
```

profile of v0, /device:TPU:1, one launch (start us, length us, event | category | flops | bytes accessed | tf_op | source)
XLA Modules:
  0.0 324.1 jit_solution(9181104681590164373)
XLA Ops:
  1.4 2.0 collective-permute-start
  4.5 1.4 collective-permute-done.1
  7.0 3.4 %collective-permute-start.2 = (f32[8,2,36]{1,2,0:T(8,128)S(1)}, f32[8,2,36]{1,2,0:T(8,128)S(1)}, u32[]{:S(2)}, u32[]{:S(2)}) collective-permute-start(f32[8,2,36]{1,2,0:T(8,128)S(1)} %get-tuple-element.48), channel_id=1, source_target_pairs={{0,4},{4,8},{8,12},{1,5},{5,9},{9,13},{2,6},{6,10},{10,14},{3,7},{... | collective-permute-start | bytes 6920 | tf_op jit(solution)/shard_map/ppermute | solution.py:19
  10.4 1.3 collective-permute-start.3
  12.7 3.8 %collective-permute-done.3 = f32[8,2,36]{1,2,0:T(8,128)S(1)} collective-permute-done((f32[8,2,36]{1,2,0:T(8,128)S(1)}, f32[8,2,36]{1,2,0:T(8,128)S(1)}, u32[]{:S(2)}, u32[]{:S(2)}) %collective-permute-start.3) | collective-permute-done | bytes 2336 | tf_op jit(solution)/shard_map/ppermute | solution.py:21
  17.4 6.3 %collective-permute-start.4 = (f32[2,68,36]{1,2,0:T(8,128)S(1)}, f32[2,68,36]{1,2,0:T(8,128)S(1)}, u32[]{:S(2)}, u32[]{:S(2)}) collective-permute-start(f32[2,68,36]{1,2,0:T(8,128)S(1)} %get-tuple-element.30), channel_id=1, source_target_pairs={{0,1},{1,2},{2,3},{4,5},{5,6},{6,7},{8,9},{9,10},{10,11},{12,13},{... | collective-permute-start | bytes 58760 | tf_op jit(solution)/shard_map/ppermute | solution.py:19
  23.7 1.9 collective-permute-start.5
  25.7 3.4 %collective-permute-done.5 = f32[2,68,36]{1,2,0:T(8,128)S(1)} collective-permute-done((f32[2,68,36]{1,2,0:T(8,128)S(1)}, f32[2,68,36]{1,2,0:T(8,128)S(1)}, u32[]{:S(2)}, u32[]{:S(2)}) %collective-permute-start.5) | collective-permute-done | bytes 19616 | tf_op jit(solution)/shard_map/ppermute | solution.py:21
  29.1 1.9 fusion.44
  31.0 1.4 fusion.149
  32.5 6.4 %copy_add_fusion = f32[32,256,128]{2,0,1:T(8,128)S(1)} fusion(f32[32,256,128]{2,1,0:T(8,128)S(1)} %copy-done.3, f32[256,12,128]{2,0,1:T(8,128)S(1)} %fusion.149, f32[12]{0:T(128)S(1)} %add_multiply_fusion.1), kind=kOutput, calls=%fused_computation.4 | convolution fusion | flops 152050816 | bytes 9961520 | tf_op jit(solution)/shard_map/tbl,st->sbl/dot_general | solution.py:50
  38.9 5.4 %fusion.2 = f32[12,256,128]{2,0,1:T(8,128)S(1)} fusion(f32[32,256,128]{2,1,0:T(8,128)S(1)} %copy-done.4, f32[32,256,128]{2,0,1:T(8,128)S(1)} %copy_add_fusion, f32[256]{0:T(256)S(1)} %multiply_cosine_fusion, f32[12]{0:T(128)S(1)} %add_multiply_fusion.1), kind=kOutput, calls=%fused_computation.3 | convolution fusion | flops 155196544 | bytes 9962544 | tf_op jit(solution)/shard_map/sbl,st->tbl/dot_general | solution.py:70
  44.3 1.6 fusion.29
  50.2 3.2 collective-permute-start.8
  53.4 1.3 collective-permute-start.9
  54.9 2.9 collective-permute-done.8
  57.8 4.4 %collective-permute-done.9 = f32[12,2,32]{1,2,0:T(8,128)S(1)} collective-permute-done((f32[12,2,32]{1,2,0:T(8,128)S(1)}, f32[12,2,32]{1,2,0:T(8,128)S(1)}, u32[]{:S(2)}, u32[]{:S(2)}) %collective-permute-start.9) | collective-permute-done | bytes 3104 | tf_op jit(solution)/shard_map/ppermute | solution.py:21
  62.3 2.4 collective-permute-start.10
  64.7 1.9 collective-permute-start.11
  66.9 3.0 collective-permute-done.11
  70.9 1.2 collective-permute-start.12
  74.7 3.2 collective-permute-start.14
  78.0 1.3 collective-permute-start.15
  79.3 2.5 collective-permute-done.14
  81.7 4.3 %collective-permute-done.15 = f32[8,2,36]{1,2,0:T(8,128)S(1)} collective-permute-done((f32[8,2,36]{1,2,0:T(8,128)S(1)}, f32[8,2,36]{1,2,0:T(8,128)S(1)}, u32[]{:S(2)}, u32[]{:S(2)}) %collective-permute-start.15) | collective-permute-done | bytes 2336 | tf_op jit(solution)/shard_map/ppermute | solution.py:21
  86.2 2.8 collective-permute-start.16
  88.9 1.9 collective-permute-start.17
  90.9 3.4 %collective-permute-done.17 = f32[2,68,36]{1,2,0:T(8,128)S(1)} collective-permute-done((f32[2,68,36]{1,2,0:T(8,128)S(1)}, f32[2,68,36]{1,2,0:T(8,128)S(1)}, u32[]{:S(2)}, u32[]{:S(2)}) %collective-permute-start.17) | collective-permute-done | bytes 19616 | tf_op jit(solution)/shard_map/ppermute | solution.py:21
  95.3 1.5 fusion.146
  96.8 4.2 %fusion.11 = f32[32,256,128]{2,0,1:T(8,128)S(1)} fusion(f32[256,12,128]{2,0,1:T(8,128)S(1)} %fusion.146, f32[12]{0:T(128)S(1)} %add_multiply_fusion.1), kind=kOutput, calls=%fused_computation.14 | convolution fusion | flops 151002240 | bytes 5767216 | tf_op jit(solution)/shard_map/tbl,st->sbl/dot_general | solution.py:50
  101.0 3.3 %fusion.6 = f32[12,256,128]{2,0,1:T(8,128)S(1)} fusion(f32[32,256,128]{2,0,1:T(8,128)S(1)} %fusion.11, f32[32,256,128]{2,0,1:T(8,128)S(1)} %copy_add_fusion, f32[256]{0:T(256)S(1)} %multiply_cosine_fusion, f32[12]{0:T(128)S(1)} %add_multiply_fusion.1), kind=kOutput, calls=%fused_computation.7 | convolution fusion | flops 155196544 | bytes 9962544 | tf_op jit(solution)/shard_map/sbl,st->tbl/dot_general | solution.py:70
  104.3 1.6 fusion.32
  105.9 1.2 fusion.215
  107.1 11.5 %collective-permute-start.18 = (f32[12,68,2]{1,2,0:T(2,128)S(1)}, f32[12,68,2]{1,2,0:T(2,128)S(1)}, u32[]{:S(2)}, u32[]{:S(2)}) collective-permute-start(f32[12,68,2]{1,2,0:T(2,128)S(1)} %get-tuple-element.34), channel_id=1, source_target_pairs={{0,16},{16,0},{1,17},{17,1},{2,18},{18,2},{3,19},{19,3},{4,20},{20... | collective-permute-start | bytes 19592 | tf_op jit(solution)/shard_map/ppermute | solution.py:19
  121.3 1.6 collective-permute-start.20
  122.9 1.3 collective-permute-start.21
  124.4 2.9 collective-permute-done.20
  127.3 4.4 %collective-permute-done.21 = f32[12,2,32]{1,2,0:T(8,128)S(1)} collective-permute-done((f32[12,2,32]{1,2,0:T(8,128)S(1)}, f32[12,2,32]{1,2,0:T(8,128)S(1)}, u32[]{:S(2)}, u32[]{:S(2)}) %collective-permute-start.21) | collective-permute-done | bytes 3104 | tf_op jit(solution)/shard_map/ppermute | solution.py:21
  131.8 2.4 collective-permute-start.22
  134.2 1.9 collective-permute-start.23
  136.4 3.0 collective-permute-done.23
  140.9 36.5 %all-reduce.12 = (f32[]{:T(128)}, f32[]{:T(128)}) all-reduce(f32[]{:T(128)} %get-tuple-element.3, f32[]{:T(128)} %get-tuple-element.2), channel_id=1, replica_groups=mesh['lon'=2,'lat'=4,'tm'=4] {'lon','lat','tm'}, use_global_device_ids=true, to_apply=%region_1.2 | all-reduce | flops 2 | bytes 16 | tf_op jit(solution)/shard_map/psum | solution.py:96
  179.4 40.9 %psum.30 = f32[]{:T(128)} all-reduce(f32[]{:T(128)} %get-tuple-element.8), channel_id=1, replica_groups=mesh['lon'=2,'lat'=4,'tm'=4] {'lon','lat','tm'}, use_global_device_ids=true, to_apply=%region_5.6 | all-reduce | flops 1 | bytes 8 | tf_op jit(solution)/shard_map/psum | solution.py:96
  221.8 2.0 collective-permute-start.24
  224.8 1.8 collective-permute-done.25
  226.7 1.6 collective-permute-start.26
  228.4 1.3 collective-permute-start.27
  230.6 3.8 %collective-permute-done.27 = f32[8,2,36]{1,2,0:T(8,128)S(1)} collective-permute-done((f32[8,2,36]{1,2,0:T(8,128)S(1)}, f32[8,2,36]{1,2,0:T(8,128)S(1)}, u32[]{:S(2)}, u32[]{:S(2)}) %collective-permute-start.27) | collective-permute-done | bytes 2336 | tf_op jit(solution)/shard_map/ppermute | solution.py:21
  234.6 7.0 %collective-permute-start.28 = (f32[2,68,36]{1,2,0:T(8,128)S(1)}, f32[2,68,36]{1,2,0:T(8,128)S(1)}, u32[]{:S(2)}, u32[]{:S(2)}) collective-permute-start(f32[2,68,36]{1,2,0:T(8,128)S(1)} %get-tuple-element.22), channel_id=1, source_target_pairs={{0,1},{1,2},{2,3},{4,5},{5,6},{6,7},{8,9},{9,10},{10,11},{12,13},{... | collective-permute-start | bytes 58760 | tf_op jit(solution)/shard_map/ppermute | solution.py:19
  241.6 1.9 collective-permute-start.29
  243.5 3.4 %collective-permute-done.29 = f32[2,68,36]{1,2,0:T(8,128)S(1)} collective-permute-done((f32[2,68,36]{1,2,0:T(8,128)S(1)}, f32[2,68,36]{1,2,0:T(8,128)S(1)}, u32[]{:S(2)}, u32[]{:S(2)}) %collective-permute-start.29) | collective-permute-done | bytes 19616 | tf_op jit(solution)/shard_map/ppermute | solution.py:21
  247.9 1.5 fusion.143
  249.4 4.2 %fusion.9 = f32[32,256,128]{2,0,1:T(8,128)S(1)} fusion(f32[256,12,128]{2,0,1:T(8,128)S(1)} %fusion.143, f32[12]{0:T(128)S(1)} %add_multiply_fusion.1), kind=kOutput, calls=%fused_computation.12 | convolution fusion | flops 151002240 | bytes 5767216 | tf_op jit(solution)/shard_map/tbl,st->sbl/dot_general | solution.py:50
  253.7 3.3 %fusion.4 = f32[12,256,128]{2,0,1:T(8,128)S(1)} fusion(f32[32,256,128]{2,0,1:T(8,128)S(1)} %fusion.9, f32[32,256,128]{2,0,1:T(8,128)S(1)} %copy-done.1, f32[256]{0:T(256)S(1)} %multiply_cosine_fusion, f32[12]{0:T(128)S(1)} %add_multiply_fusion.1), kind=kOutput, calls=%fused_computation.5 | convolution fusion | flops 155196544 | bytes 9962544 | tf_op jit(solution)/shard_map/sbl,st->tbl/dot_general | solution.py:70
  256.9 1.6 fusion.35
  258.5 1.2 fusion.212
  263.0 2.4 collective-permute-start.32
  265.4 1.3 collective-permute-start.33
  266.9 2.9 collective-permute-done.32
  269.8 4.2 %collective-permute-done.33 = f32[12,2,32]{1,2,0:T(8,128)S(1)} collective-permute-done((f32[12,2,32]{1,2,0:T(8,128)S(1)}, f32[12,2,32]{1,2,0:T(8,128)S(1)}, u32[]{:S(2)}, u32[]{:S(2)}) %collective-permute-start.33) | collective-permute-done | bytes 3104 | tf_op jit(solution)/shard_map/ppermute | solution.py:21
  274.1 2.6 collective-permute-start.34
  276.7 1.9 collective-permute-start.35
  278.9 3.0 collective-permute-done.35
  283.4 38.4 %psum.31 = f32[]{:T(128)} all-reduce(f32[]{:T(128)} %get-tuple-element.6), channel_id=1, replica_groups=mesh['lon'=2,'lat'=4,'tm'=4] {'lon','lat','tm'}, use_global_device_ids=true, to_apply=%region_7.8 | all-reduce | flops 1 | bytes 8 | tf_op jit(solution)/shard_map/psum | solution.py:96
  (99 shorter events, 28.8 us)
Async XLA Ops:
  1.4 3.1 collective-permute-start
  3.4 2.5 collective-permute-start.1
  4.4 28.0 %copy-start.3 = (f32[32,256,128]{2,1,0:T(8,128)S(1)}, f32[32,256,128]{2,1,0:T(8,128)}, u32[]{:S(2)}) copy-start(f32[32,256,128]{2,1,0:T(8,128)} %param.5) | copy-start | bytes 12582916
  7.0 5.7 %collective-permute-start.2 = (f32[8,2,36]{1,2,0:T(8,128)S(1)}, f32[8,2,36]{1,2,0:T(8,128)S(1)}, u32[]{:S(2)}, u32[]{:S(2)}) collective-permute-start(f32[8,2,36]{1,2,0:T(8,128)S(1)} %get-tuple-element.48), channel_id=1, source_target_pairs={{0,4},{4,8},{8,12},{1,5},{5,9},{9,13},{2,6},{6,10},{10,14},{3,7},{... | collective-permute-start | bytes 6920 | tf_op jit(solution)/shard_map/ppermute | solution.py:19
  10.4 6.1 %collective-permute-start.3 = (f32[8,2,36]{1,2,0:T(8,128)S(1)}, f32[8,2,36]{1,2,0:T(8,128)S(1)}, u32[]{:S(2)}, u32[]{:S(2)}) collective-permute-start(f32[8,2,36]{1,2,0:T(8,128)S(1)} %get-tuple-element.49), channel_id=1, source_target_pairs={{4,0},{8,4},{12,8},{5,1},{9,5},{13,9},{6,2},{10,6},{14,10},{7,3},{... | collective-permute-start | bytes 6920 | tf_op jit(solution)/shard_map/ppermute | solution.py:21
  17.4 8.3 %collective-permute-start.4 = (f32[2,68,36]{1,2,0:T(8,128)S(1)}, f32[2,68,36]{1,2,0:T(8,128)S(1)}, u32[]{:S(2)}, u32[]{:S(2)}) collective-permute-start(f32[2,68,36]{1,2,0:T(8,128)S(1)} %get-tuple-element.30), channel_id=1, source_target_pairs={{0,1},{1,2},{2,3},{4,5},{5,6},{6,7},{8,9},{9,10},{10,11},{12,13},{... | collective-permute-start | bytes 58760 | tf_op jit(solution)/shard_map/ppermute | solution.py:19
  23.7 5.3 %collective-permute-start.5 = (f32[2,68,36]{1,2,0:T(8,128)S(1)}, f32[2,68,36]{1,2,0:T(8,128)S(1)}, u32[]{:S(2)}, u32[]{:S(2)}) collective-permute-start(f32[2,68,36]{1,2,0:T(8,128)S(1)} %get-tuple-element.31), channel_id=1, source_target_pairs={{1,0},{2,1},{3,2},{5,4},{6,5},{7,6},{9,8},{10,9},{11,10},{13,12},{... | collective-permute-start | bytes 58760 | tf_op jit(solution)/shard_map/ppermute | solution.py:21
  32.5 6.4 %copy-start.4 = (f32[32,256,128]{2,1,0:T(8,128)S(1)}, f32[32,256,128]{2,1,0:T(8,128)}, u32[]{:S(2)}) copy-start(f32[32,256,128]{2,1,0:T(8,128)} %param.4) | copy-start | bytes 12582916
  38.9 62.1 %copy-start = (f32[32,256,128]{2,0,1:T(8,128)}, f32[32,256,128]{2,0,1:T(8,128)S(1)}, u32[]{:S(2)}) copy-start(f32[32,256,128]{2,0,1:T(8,128)S(1)} %copy_add_fusion) | copy-start | bytes 12582916
  38.9 15.8 %copy-start.2 = (f32[8,64,32]{1,2,0:T(8,128)S(1)}, f32[8,64,32]{1,2,0:T(8,128)}, u32[]{:S(2)}) copy-start(f32[8,64,32]{1,2,0:T(8,128)} %param.6) | copy-start | bytes 196612
  44.3 26.0 %copy-start.7 = (pred[64]{0:T(512)(128)(4,1)S(1)}, pred[64]{0:T(512)(128)(4,1)}, u32[]{:S(2)}) copy-start(pred[64]{0:T(512)(128)(4,1)} %constant.85.clone.1) | copy-start | bytes 196
  44.3 26.2 %copy-start.5 = (f32[8,64,32]{1,2,0:T(8,128)S(1)}, f32[8,64,32]{1,2,0:T(8,128)}, u32[]{:S(2)}) copy-start(f32[8,64,32]{1,2,0:T(8,128)} %param.7) | copy-start | bytes 196612
  44.3 26.2 %copy-start.6 = (pred[8]{0:T(512)(128)(4,1)S(1)}, pred[8]{0:T(512)(128)(4,1)}, u32[]{:S(2)}) copy-start(pred[8]{0:T(512)(128)(4,1)} %constant.86.clone.1) | copy-start | bytes 28
  47.1 2.6 collective-permute-start.6
  47.5 2.5 collective-permute-start.7
  50.2 7.6 %collective-permute-start.8 = (f32[12,2,32]{1,2,0:T(8,128)S(1)}, f32[12,2,32]{1,2,0:T(8,128)S(1)}, u32[]{:S(2)}, u32[]{:S(2)}) collective-permute-start(f32[12,2,32]{1,2,0:T(8,128)S(1)} %get-tuple-element.42), channel_id=1, source_target_pairs={{0,4},{4,8},{8,12},{1,5},{5,9},{9,13},{2,6},{6,10},{10,14},{3,7},{... | collective-permute-start | bytes 9224 | tf_op jit(solution)/shard_map/ppermute | solution.py:19
  53.4 8.7 %collective-permute-start.9 = (f32[12,2,32]{1,2,0:T(8,128)S(1)}, f32[12,2,32]{1,2,0:T(8,128)S(1)}, u32[]{:S(2)}, u32[]{:S(2)}) collective-permute-start(f32[12,2,32]{1,2,0:T(8,128)S(1)} %get-tuple-element.43), channel_id=1, source_target_pairs={{4,0},{8,4},{12,8},{5,1},{9,5},{13,9},{6,2},{10,6},{14,10},{7,3},{... | collective-permute-start | bytes 9224 | tf_op jit(solution)/shard_map/ppermute | solution.py:21
  62.3 4.6 %collective-permute-start.10 = (f32[2,72,32]{1,2,0:T(8,128)S(1)}, f32[2,72,32]{1,2,0:T(8,128)S(1)}, u32[]{:S(2)}, u32[]{:S(2)}) collective-permute-start(f32[2,72,32]{1,2,0:T(8,128)S(1)} %get-tuple-element.18), channel_id=1, source_target_pairs={{0,1},{1,2},{2,3},{4,5},{5,6},{6,7},{8,9},{9,10},{10,11},{12,13},{... | collective-permute-start | bytes 55304 | tf_op jit(solution)/shard_map/ppermute | solution.py:19
  64.7 5.2 %collective-permute-start.11 = (f32[2,72,32]{1,2,0:T(8,128)S(1)}, f32[2,72,32]{1,2,0:T(8,128)S(1)}, u32[]{:S(2)}, u32[]{:S(2)}) collective-permute-start(f32[2,72,32]{1,2,0:T(8,128)S(1)} %get-tuple-element.19), channel_id=1, source_target_pairs={{1,0},{2,1},{3,2},{5,4},{6,5},{7,6},{9,8},{10,9},{11,10},{13,12},{... | collective-permute-start | bytes 55304 | tf_op jit(solution)/shard_map/ppermute | solution.py:21
  70.9 2.7 collective-permute-start.12
  72.1 2.5 collective-permute-start.13
  74.7 7.0 %collective-permute-start.14 = (f32[8,2,36]{1,2,0:T(8,128)S(1)}, f32[8,2,36]{1,2,0:T(8,128)S(1)}, u32[]{:S(2)}, u32[]{:S(2)}) collective-permute-start(f32[8,2,36]{1,2,0:T(8,128)S(1)} %get-tuple-element.46), channel_id=1, source_target_pairs={{0,4},{4,8},{8,12},{1,5},{5,9},{9,13},{2,6},{6,10},{10,14},{3,7},{... | collective-permute-start | bytes 6920 | tf_op jit(solution)/shard_map/ppermute | solution.py:19
  78.0 8.1 %collective-permute-start.15 = (f32[8,2,36]{1,2,0:T(8,128)S(1)}, f32[8,2,36]{1,2,0:T(8,128)S(1)}, u32[]{:S(2)}, u32[]{:S(2)}) collective-permute-start(f32[8,2,36]{1,2,0:T(8,128)S(1)} %get-tuple-element.47), channel_id=1, source_target_pairs={{4,0},{8,4},{12,8},{5,1},{9,5},{13,9},{6,2},{10,6},{14,10},{7,3},{... | collective-permute-start | bytes 6920 | tf_op jit(solution)/shard_map/ppermute | solution.py:21
  86.2 4.7 %collective-permute-start.16 = (f32[2,68,36]{1,2,0:T(8,128)S(1)}, f32[2,68,36]{1,2,0:T(8,128)S(1)}, u32[]{:S(2)}, u32[]{:S(2)}) collective-permute-start(f32[2,68,36]{1,2,0:T(8,128)S(1)} %get-tuple-element.26), channel_id=1, source_target_pairs={{0,1},{1,2},{2,3},{4,5},{5,6},{6,7},{8,9},{9,10},{10,11},{12,13},{... | collective-permute-start | bytes 58760 | tf_op jit(solution)/shard_map/ppermute | solution.py:19
  88.9 5.3 %collective-permute-start.17 = (f32[2,68,36]{1,2,0:T(8,128)S(1)}, f32[2,68,36]{1,2,0:T(8,128)S(1)}, u32[]{:S(2)}, u32[]{:S(2)}) collective-permute-start(f32[2,68,36]{1,2,0:T(8,128)S(1)} %get-tuple-element.27), channel_id=1, source_target_pairs={{1,0},{2,1},{3,2},{5,4},{6,5},{7,6},{9,8},{10,9},{11,10},{13,12},{... | collective-permute-start | bytes 58760 | tf_op jit(solution)/shard_map/ppermute | solution.py:21
  107.1 13.7 %collective-permute-start.18 = (f32[12,68,2]{1,2,0:T(2,128)S(1)}, f32[12,68,2]{1,2,0:T(2,128)S(1)}, u32[]{:S(2)}, u32[]{:S(2)}) collective-permute-start(f32[12,68,2]{1,2,0:T(2,128)S(1)} %get-tuple-element.34), channel_id=1, source_target_pairs={{0,16},{16,0},{1,17},{17,1},{2,18},{18,2},{3,19},{19,3},{4,20},{20... | collective-permute-start | bytes 19592 | tf_op jit(solution)/shard_map/ppermute | solution.py:19
  118.6 2.5 collective-permute-start.19
  121.3 6.0 %collective-permute-start.20 = (f32[12,2,32]{1,2,0:T(8,128)S(1)}, f32[12,2,32]{1,2,0:T(8,128)S(1)}, u32[]{:S(2)}, u32[]{:S(2)}) collective-permute-start(f32[12,2,32]{1,2,0:T(8,128)S(1)} %get-tuple-element.40), channel_id=1, source_target_pairs={{0,4},{4,8},{8,12},{1,5},{5,9},{9,13},{2,6},{6,10},{10,14},{3,7},{... | collective-permute-start | bytes 9224 | tf_op jit(solution)/shard_map/ppermute | solution.py:19
  122.9 8.8 %collective-permute-start.21 = (f32[12,2,32]{1,2,0:T(8,128)S(1)}, f32[12,2,32]{1,2,0:T(8,128)S(1)}, u32[]{:S(2)}, u32[]{:S(2)}) collective-permute-start(f32[12,2,32]{1,2,0:T(8,128)S(1)} %get-tuple-element.41), channel_id=1, source_target_pairs={{4,0},{8,4},{12,8},{5,1},{9,5},{13,9},{6,2},{10,6},{14,10},{7,3},{... | collective-permute-start | bytes 9224 | tf_op jit(solution)/shard_map/ppermute | solution.py:21
  131.8 4.6 %collective-permute-start.22 = (f32[2,72,32]{1,2,0:T(8,128)S(1)}, f32[2,72,32]{1,2,0:T(8,128)S(1)}, u32[]{:S(2)}, u32[]{:S(2)}) collective-permute-start(f32[2,72,32]{1,2,0:T(8,128)S(1)} %get-tuple-element.16), channel_id=1, source_target_pairs={{0,1},{1,2},{2,3},{4,5},{5,6},{6,7},{8,9},{9,10},{10,11},{12,13},{... | collective-permute-start | bytes 55304 | tf_op jit(solution)/shard_map/ppermute | solution.py:19
  134.2 5.2 %collective-permute-start.23 = (f32[2,72,32]{1,2,0:T(8,128)S(1)}, f32[2,72,32]{1,2,0:T(8,128)S(1)}, u32[]{:S(2)}, u32[]{:S(2)}) collective-permute-start(f32[2,72,32]{1,2,0:T(8,128)S(1)} %get-tuple-element.17), channel_id=1, source_target_pairs={{1,0},{2,1},{3,2},{5,4},{6,5},{7,6},{9,8},{10,9},{11,10},{13,12},{... | collective-permute-start | bytes 55304 | tf_op jit(solution)/shard_map/ppermute | solution.py:21
  221.8 3.1 collective-permute-start.24
  223.8 2.8 collective-permute-start.25
  226.7 3.9 %collective-permute-start.26 = (f32[8,2,36]{1,2,0:T(8,128)S(1)}, f32[8,2,36]{1,2,0:T(8,128)S(1)}, u32[]{:S(2)}, u32[]{:S(2)}) collective-permute-start(f32[8,2,36]{1,2,0:T(8,128)S(1)} %get-tuple-element.44), channel_id=1, source_target_pairs={{0,4},{4,8},{8,12},{1,5},{5,9},{9,13},{2,6},{6,10},{10,14},{3,7},{... | collective-permute-start | bytes 6920 | tf_op jit(solution)/shard_map/ppermute | solution.py:19
  228.4 6.1 %collective-permute-start.27 = (f32[8,2,36]{1,2,0:T(8,128)S(1)}, f32[8,2,36]{1,2,0:T(8,128)S(1)}, u32[]{:S(2)}, u32[]{:S(2)}) collective-permute-start(f32[8,2,36]{1,2,0:T(8,128)S(1)} %get-tuple-element.45), channel_id=1, source_target_pairs={{4,0},{8,4},{12,8},{5,1},{9,5},{13,9},{6,2},{10,6},{14,10},{7,3},{... | collective-permute-start | bytes 6920 | tf_op jit(solution)/shard_map/ppermute | solution.py:21
  234.6 9.0 %collective-permute-start.28 = (f32[2,68,36]{1,2,0:T(8,128)S(1)}, f32[2,68,36]{1,2,0:T(8,128)S(1)}, u32[]{:S(2)}, u32[]{:S(2)}) collective-permute-start(f32[2,68,36]{1,2,0:T(8,128)S(1)} %get-tuple-element.22), channel_id=1, source_target_pairs={{0,1},{1,2},{2,3},{4,5},{5,6},{6,7},{8,9},{9,10},{10,11},{12,13},{... | collective-permute-start | bytes 58760 | tf_op jit(solution)/shard_map/ppermute | solution.py:19
  241.6 5.3 %collective-permute-start.29 = (f32[2,68,36]{1,2,0:T(8,128)S(1)}, f32[2,68,36]{1,2,0:T(8,128)S(1)}, u32[]{:S(2)}, u32[]{:S(2)}) collective-permute-start(f32[2,68,36]{1,2,0:T(8,128)S(1)} %get-tuple-element.23), channel_id=1, source_target_pairs={{1,0},{2,1},{3,2},{5,4},{6,5},{7,6},{9,8},{10,9},{11,10},{13,12},{... | collective-permute-start | bytes 58760 | tf_op jit(solution)/shard_map/ppermute | solution.py:21
  247.9 5.7 %copy-start.1 = (f32[32,256,128]{2,0,1:T(8,128)S(1)}, f32[32,256,128]{2,0,1:T(8,128)}, u32[]{:S(2)}) copy-start(f32[32,256,128]{2,0,1:T(8,128)} %copy-done) | copy-start | bytes 12582916
  259.8 2.8 collective-permute-start.30
  260.3 2.5 collective-permute-start.31
  263.0 6.8 %collective-permute-start.32 = (f32[12,2,32]{1,2,0:T(8,128)S(1)}, f32[12,2,32]{1,2,0:T(8,128)S(1)}, u32[]{:S(2)}, u32[]{:S(2)}) collective-permute-start(f32[12,2,32]{1,2,0:T(8,128)S(1)} %get-tuple-element.38), channel_id=1, source_target_pairs={{0,4},{4,8},{8,12},{1,5},{5,9},{9,13},{2,6},{6,10},{10,14},{3,7},{... | collective-permute-start | bytes 9224 | tf_op jit(solution)/shard_map/ppermute | solution.py:19
  265.4 8.6 %collective-permute-start.33 = (f32[12,2,32]{1,2,0:T(8,128)S(1)}, f32[12,2,32]{1,2,0:T(8,128)S(1)}, u32[]{:S(2)}, u32[]{:S(2)}) collective-permute-start(f32[12,2,32]{1,2,0:T(8,128)S(1)} %get-tuple-element.39), channel_id=1, source_target_pairs={{4,0},{8,4},{12,8},{5,1},{9,5},{13,9},{6,2},{10,6},{14,10},{7,3},{... | collective-permute-start | bytes 9224 | tf_op jit(solution)/shard_map/ppermute | solution.py:21
  274.1 4.8 %collective-permute-start.34 = (f32[2,72,32]{1,2,0:T(8,128)S(1)}, f32[2,72,32]{1,2,0:T(8,128)S(1)}, u32[]{:S(2)}, u32[]{:S(2)}) collective-permute-start(f32[2,72,32]{1,2,0:T(8,128)S(1)} %get-tuple-element.14), channel_id=1, source_target_pairs={{0,1},{1,2},{2,3},{4,5},{5,6},{6,7},{8,9},{9,10},{10,11},{12,13},{... | collective-permute-start | bytes 55304 | tf_op jit(solution)/shard_map/ppermute | solution.py:19
  276.7 5.2 %collective-permute-start.35 = (f32[2,72,32]{1,2,0:T(8,128)S(1)}, f32[2,72,32]{1,2,0:T(8,128)S(1)}, u32[]{:S(2)}, u32[]{:S(2)}) collective-permute-start(f32[2,72,32]{1,2,0:T(8,128)S(1)} %get-tuple-element.15), channel_id=1, source_target_pairs={{1,0},{2,1},{3,2},{5,4},{6,5},{7,6},{9,8},{10,9},{11,10},{13,12},{... | collective-permute-start | bytes 55304 | tf_op jit(solution)/shard_map/ppermute | solution.py:21
where the time goes:
time: 330 us; the launch traced here: 324 us
  blocking collectives  116 us (35%)
  starting transfers between devices  80 us (24%)
  waiting for transfers between devices  67.6 us (20%)
  matrix products  43.5 us (13%)
  other arithmetic  8.67 us (3%)
  between operations  5.66 us (2%)
    psum x3, blocking collectives, global_sum(): return lax.psum(values, ('lon', 'lat', 'tm'))  116 us
    ppermute x18, starting transfers between devices, with_halo(): lax.ppermute(tail, axis, [(i, (i + 1) % count) for i in range(ends)])  56.7 us
    ppermute x18, waiting for transfers between devices, with_halo(): lax.ppermute(head, axis, [((i + 1) % count, i) for i in range(ends)])  49.2 us
    ppermute x18, starting transfers between devices, with_halo(): lax.ppermute(head, axis, [((i + 1) % count, i) for i in range(ends)])  23.2 us
    ppermute x18, waiting for transfers between devices, with_halo(): lax.ppermute(tail, axis, [(i, (i + 1) % count) for i in range(ends)])  18.4 us
    dot_general x3, matrix products, evaluate(): return jnp.einsum('tbl,st->sbl', partial_value, time_tab, precision=highest)  14.9 us
    dot_general x3, matrix products, adjoint(): jnp.einsum('sbl,st->tbl', cell_values, time_tab, precision=highest)  11.9 us
  transfers between devices with their start and end apart: 36, of which 29 were waited for; matrix products, arithmetic and copies ran while one was open for 1% of the time, Pallas kernels for 0%

commit v1 on v0

v1 whole, which is shorter than its diff:
```python
import functools

import numpy as np
import jax
import jax.numpy as jnp
from jax import lax
from jax.experimental import pallas as pl
from jax.experimental.pallas import tpu as pltpu
from jax.sharding import PartitionSpec as P

tweedie_power = 1.6
smooth = 0.5
bf16 = jnp.bfloat16
f32 = jnp.float32
LANES = 128
LEAD = 8
AXES = ("lon", "lat", "tm")


def spline(offsets):
    distance = np.abs(np.asarray(offsets, np.float64))
    near_part = (4.0 - 6.0 * distance**2 + 3.0 * distance**3) / 6.0
    far_part = np.maximum(2.0 - distance, 0.0) ** 3 / 6.0
    return np.where(distance < 1.0, near_part, far_part)


def halves(table):
    high = table.astype(np.float32).astype(bf16)
    low = (table - high.astype(np.float64)).astype(np.float32).astype(bf16)
    return high, low


def lat_tables(count):
    knots = np.arange(count + 2 * LEAD) - LEAD
    cells = np.arange(4 * count)
    high, low = halves(spline((cells[:, None] - 4.0 * knots[None, :] - 1.5) / 4.0))
    forward = np.concatenate([high, high, low], axis=1)
    back = np.concatenate([high.T, low.T], axis=0)
    return forward, back


def lon_tables(count):
    lanes = np.arange(LANES)
    knots = np.where(lanes >= LANES - 2, lanes - LANES, lanes)
    valid = knots < count + 2
    cells = np.arange(4 * count)
    table = spline((cells[:, None] - 4.0 * knots[None, :] - 1.5) / 4.0) * valid[None, :]
    high, low = halves(table)
    gap = count + 8
    forward = (
        high.T.astype(np.float32)
        + np.roll(high.T.astype(np.float32), gap, 0)
        + np.roll(low.T.astype(np.float32), 2 * gap, 0)
    ).astype(bf16)
    return forward, high, low


def area_table(lat_total):
    index = np.arange(lat_total, dtype=np.float32)
    degrees = np.float32(90.0) - (index + np.float32(0.5)) * np.float32(180.0) / np.float32(lat_total)
    values = np.cos((degrees * np.float32(np.pi / 180.0)).astype(np.float64)).astype(np.float32)
    return np.ascontiguousarray(np.broadcast_to(values[:, None], (lat_total, LANES)))


def time_taps():
    taps = []
    for phase in range(4):
        row = []
        for shift in range(-2, 3):
            weight = float(spline((phase - 4.0 * shift - 1.5) / 4.0))
            if weight != 0.0:
                row.append((shift + 2, weight))
        taps.append(row)
    return taps


def split(values):
    high = values.astype(bf16)
    return high, (values - high.astype(f32)).astype(bf16)


def kernel(
    counts,
    mesh_sizes,
    coef_ref,
    inv_ref,
    area_hbm,
    offset_hbm,
    precip_hbm,
    lon_fwd,
    lat_fwd,
    lat_back,
    lon_high,
    lon_low,
    step_ref,
    resid_ref,
    weight,
    precip,
    area,
    cells,
    coef,
    inv,
    res,
    dir0,
    dir1,
    img0,
    img1,
    lon_send,
    lon_recv,
    lat_send,
    lat_recv,
    tm_send,
    tm_recv,
    sum_lon,
    sum_lat,
    sum_tm,
    load_sem,
    lon_sems,
    lat_sems,
    tm_sems,
    sum_lon_sems,
    sum_lat_sems,
    sum_tm_sems,
):
    time_n, lat_n, lon_n = counts
    padded_time = time_n + 4
    rows = lat_n + 2 * LEAD
    half = LANES // 2
    own_t = slice(2, 2 + time_n)
    own_a = slice(LEAD, LEAD + lat_n)
    me = {name: lax.axis_index(name) for name in AXES}
    size = dict(zip(AXES, mesh_sizes))
    pending = []

    lat_cells = 4 * lat_n
    loads = [
        pltpu.make_async_copy(
            area_hbm.at[pl.ds(pl.multiple_of(me["lat"] * lat_cells, lat_cells), lat_cells)],
            area,
            load_sem.at[0],
        )
    ]
    part = 2 * time_n
    for i in range(2):
        span = pl.ds(i * part, part)
        loads.append(pltpu.make_async_copy(offset_hbm.at[span], weight.at[span], load_sem.at[1 + 2 * i]))
        loads.append(pltpu.make_async_copy(precip_hbm.at[span], precip.at[span], load_sem.at[2 + 2 * i]))
    for load in loads:
        load.start()

    barrier = pltpu.get_barrier_semaphore()
    for name in AXES:
        for hop in range(1, size[name]):
            pl.semaphore_signal(
                barrier,
                inc=1,
                device_id={name: lax.rem(me[name] + hop, size[name])},
                device_id_type=pl.DeviceIdType.MESH,
            )

    coef[...] = jnp.zeros(coef.shape, f32)
    inv[...] = jnp.zeros(inv.shape, f32)
    coef[own_t, own_a, 0:lon_n] = coef_ref[...]
    inv[own_t, own_a, 0:lon_n] = inv_ref[...]
    pl.semaphore_wait(barrier, sum(size[name] - 1 for name in AXES))

    lane = lax.broadcasted_iota(jnp.int32, (rows, LANES), 1)
    low_lanes = (lane < 2) | (lane >= LANES - 2)
    high_lanes = (lane >= lon_n - 2) & (lane < lon_n + 2)
    used_lanes = (lane < lon_n + 2) | (lane >= LANES - 2)
    own_lanes = lane[0:lat_n] < lon_n

    def remote(src, dst, sems, at, name, to):
        return pltpu.make_async_remote_copy(
            src_ref=src,
            dst_ref=dst,
            send_sem=sems.at[0, at],
            recv_sem=sems.at[1, at],
            device_id={name: to},
            device_id_type=pl.DeviceIdType.MESH,
        )

    def neighbours(name):
        count = size[name]
        return lax.rem(me[name] + count - 1, count), lax.rem(me[name] + 1, count)

    def exchange(pairs, hooks):
        copies = []
        before, after = neighbours("lon")
        for ref, bank in pairs:
            packed = jnp.zeros((rows, LANES), f32)
            for t in range(padded_time):
                slab = ref[t]
                at = 4 * t
                packed = jnp.where(
                    (lane >= at) & (lane < at + 4), pltpu.roll(slab, (at + 2) % LANES, 1), packed
                )
                at = half + 4 * t
                packed = jnp.where(
                    (lane >= at) & (lane < at + 4),
                    pltpu.roll(slab, (at - lon_n + 2) % LANES, 1),
                    packed,
                )
            full = jnp.concatenate([packed, jnp.zeros((LANES - rows, LANES), f32)], axis=0)
            lon_send[bank] = full.T
            low = pl.ds(0, 4 * padded_time)
            high = pl.ds(half, 4 * padded_time)
            down = remote(
                lon_send.at[bank, low], lon_recv.at[bank, high], lon_sems, 2 * bank, "lon", before
            )
            up = remote(
                lon_send.at[bank, high], lon_recv.at[bank, low], lon_sems, 2 * bank + 1, "lon", after
            )
            down.start()
            up.start()
            copies.append((down, up))
            pending.append((None, down))
            pending.append((None, up))
        hooks[0]()
        for (ref, bank), (down, up) in zip(pairs, copies):
            down.wait_recv()
            up.wait_recv()
            back = lon_recv[bank].T[0:rows]
            for t in range(padded_time):
                at = 4 * t
                mine = jnp.where(low_lanes, pltpu.roll(back, (LANES - at - 2) % LANES, 1), 0.0)
                at = half + 4 * t
                mine = jnp.where(high_lanes, pltpu.roll(back, (LANES - at + lon_n - 2) % LANES, 1), mine)
                ref[t] = ref[t] + mine

        def ends(name, send, recv, sems, load, store, hook):
            before, after = neighbours(name)
            has_low = me[name] > 0
            has_high = me[name] < size[name] - 1
            copies = []
            for ref, bank in pairs:
                load(ref, bank)
                down = remote(send.at[bank, 0], recv.at[bank, 1], sems, 2 * bank, name, before)
                up = remote(send.at[bank, 1], recv.at[bank, 0], sems, 2 * bank + 1, name, after)
                pl.when(has_low)(down.start)
                pl.when(has_high)(up.start)
                copies.append((down, up))
                pending.append((has_low, down))
                pending.append((has_high, up))
            hook()
            for (ref, bank), (down, up) in zip(pairs, copies):

                @pl.when(has_low)
                def _():
                    up.wait_recv()
                    store(ref, bank, 0)

                @pl.when(has_high)
                def _():
                    down.wait_recv()
                    store(ref, bank, 1)

        starts = (LEAD - 2, LEAD + lat_n - 2)

        def lat_load(ref, bank):
            for t in range(padded_time):
                for side, start in enumerate(starts):
                    lat_send[bank, side, 4 * t : 4 * t + 4] = ref[t, start : start + 4]

        def lat_store(ref, bank, side):
            start = starts[side]
            for t in range(padded_time):
                ref[t, start : start + 4] = (
                    ref[t, start : start + 4] + lat_recv[bank, side, 4 * t : 4 * t + 4]
                )

        ends("lat", lat_send, lat_recv, lat_sems, lat_load, lat_store, hooks[1])

        def tm_load(ref, bank):
            for side, start in enumerate((0, time_n)):
                for i in range(2):
                    tm_send[bank, side, i] = ref[start + 2 * i] + pltpu.roll(
                        ref[start + 2 * i + 1], half, 1
                    )

        def tm_store(ref, bank, side):
            start = (0, time_n)[side]
            for i in range(2):
                got = tm_recv[bank, side, i]
                ref[start + 2 * i] = ref[start + 2 * i] + jnp.where(used_lanes, got, 0.0)
                ref[start + 2 * i + 1] = ref[start + 2 * i + 1] + jnp.where(
                    used_lanes, pltpu.roll(got, half, 1), 0.0
                )

        ends("tm", tm_send, tm_recv, tm_sems, tm_load, tm_store, hooks[2])

    slots = {"lon": sum_lon, "lat": sum_lat, "tm": sum_tm}
    slot_sems = {"lon": sum_lon_sems, "lat": sum_lat_sems, "tm": sum_tm_sems}

    class Total:
        def __init__(self, bank, value):
            self.bank, self.value, self.stage = bank, value, 0
            self.send()

        def send(self):
            name = AXES[self.stage]
            count = size[name]
            buf = slots[name]
            buf[self.bank, me[name]] = self.value
            self.copies = []
            for hop in range(1, count):
                at = self.bank * count + hop
                mine = buf.at[self.bank, me[name]]
                out = remote(mine, mine, slot_sems[name], at, name, lax.rem(me[name] + hop, count))
                out.start()
                pending.append((None, out))
                theirs = buf.at[self.bank, lax.rem(me[name] + count - hop, count)]
                self.copies.append(
                    remote(theirs, theirs, slot_sems[name], at, name, lax.rem(me[name] + hop, count))
                )

        def advance(self):
            name = AXES[self.stage]
            for copy in self.copies:
                copy.wait_recv()
            value = slots[name][self.bank, 0]
            for i in range(1, size[name]):
                value = value + slots[name][self.bank, i]
            self.value = value
            self.stage += 1
            if self.stage < len(AXES):
                self.send()

        def read(self, first):
            tile = self.value[8 * first : 8 * first + 8]
            return jnp.sum(jnp.sum(tile, axis=0, keepdims=True), axis=1, keepdims=True)

    def tile_of(values):
        return jnp.sum(values.reshape(-1, 8, LANES), axis=0)

    def own_tile(left, right):
        masked = jnp.where(own_lanes[None], left[own_t, own_a] * right[own_t, own_a], 0.0)
        return tile_of(masked)

    taps = time_taps()

    def synth(z, m, phase):
        total = None
        for at, factor in taps[phase]:
            term = z[m + at] * factor
            total = term if total is None else total + term
        return total

    def columns(t):
        return slice(LANES * t, LANES * (t + 1))

    def apply(vec, image, cell_values, hooks):
        gap = lon_n + 8
        for pair in range(padded_time // 2):
            values = vec[2 * pair : 2 * pair + 2].reshape(2 * rows, LANES)
            high = values.astype(bf16).astype(f32)
            low = values - high
            stacked = (high + pltpu.roll(low, gap, 1) + pltpu.roll(high, 2 * gap, 1)).astype(bf16)
            wide = jnp.dot(stacked, lon_fwd[...], preferred_element_type=f32)
            high, low = split(jnp.concatenate([wide[0:rows], wide[rows:]], axis=1))
            stacked = jnp.concatenate([high, low, high], axis=0)
            cells[:, 2 * LANES * pair : 2 * LANES * (pair + 1)] = jnp.dot(
                lat_fwd[...], stacked, preferred_element_type=f32
            )
        hooks[0]()

        def group(g, carry):
            at = pl.ds(pl.multiple_of(g * 8, 8), 8)
            z = [cells[at, columns(t)] for t in range(padded_time)]
            sums = [None] * padded_time
            for m in range(time_n):
                for phase in range(4):
                    value = cell_values(4 * m + phase, at, synth(z, m, phase))
                    for shift, factor in taps[phase]:
                        term = value * factor
                        old = sums[m + shift]
                        sums[m + shift] = term if old is None else old + term
                cells[at, columns(m)] = sums[m]
            for t in range(time_n, padded_time):
                cells[at, columns(t)] = sums[t]
            return carry

        lax.fori_loop(0, lat_cells // 8, group, 0)
        hooks[1]()
        for pair in range(padded_time // 2):
            high, low = split(cells[:, 2 * LANES * pair : 2 * LANES * (pair + 1)])
            both = jnp.dot(lat_back[...], high, preferred_element_type=f32)
            rest = jnp.dot(lat_back[0:rows], low, preferred_element_type=f32)
            knots = both[0:rows] + both[rows:] + rest
            high, low = split(jnp.concatenate([knots[:, 0:LANES], knots[:, LANES:]], axis=0))
            out = (
                jnp.dot(high, lon_high[...], preferred_element_type=f32)
                + jnp.dot(low, lon_high[...], preferred_element_type=f32)
                + jnp.dot(high, lon_low[...], preferred_element_type=f32)
            )
            image[2 * pair] = out[0:rows]
            image[2 * pair + 1] = out[rows:]
        for t in range(2, 2 + time_n):
            mid = vec[t, own_a]
            outer = vec[t - 2, own_a] + vec[t + 2, own_a]
            inner = vec[t - 1, own_a] + vec[t + 1, own_a]
            outer = outer + vec[t, LEAD - 2 : LEAD + lat_n - 2] + vec[t, LEAD + 2 : LEAD + lat_n + 2]
            inner = inner + vec[t, LEAD - 1 : LEAD + lat_n - 1] + vec[t, LEAD + 1 : LEAD + lat_n + 1]
            outer = outer + pltpu.roll(mid, 2, 1) + pltpu.roll(mid, LANES - 2, 1)
            inner = inner + pltpu.roll(mid, 1, 1) + pltpu.roll(mid, LANES - 1, 1)
            bent = smooth * (18.0 * mid - 4.0 * inner + outer)
            image[t, own_a] = image[t, own_a] + jnp.where(own_lanes, bent, 0.0)
        hooks[2]()

    def nothing():
        pass

    idle = (nothing, nothing, nothing)

    def gradient_cells(s, at, value):
        linear = weight[s, at] + value
        scale = area[at]
        rate = scale * jnp.exp((2.0 - tweedie_power) * linear)
        tilted = scale * jnp.exp((1.0 - tweedie_power) * linear)
        weight[s, at] = rate
        return rate - precip[s, at] * tilted

    def weighted_cells(s, at, value):
        return weight[s, at] * value

    exchange(((coef, 0), (inv, 1)), idle)
    for load in loads:
        load.wait()
    apply(coef, img0, gradient_cells, idle)
    exchange(((img0, 2),), idle)
    res[...] = -img0[...]
    dir0[...] = inv[...] * res[...]
    first_norm = own_tile(res, dir0)

    apply(dir0, img0, weighted_cells, idle)
    sums = Total(0, jnp.concatenate([first_norm, tile_of(dir0[...] * img0[...])], axis=0))
    exchange(((img0, 3),), (sums.advance,) * 3)
    norm = sums.read(0)
    first_step = norm / sums.read(1)
    res[...] = res[...] - first_step[None] * img0[...]
    dir1[...] = inv[...] * res[...]
    tile = own_tile(res, dir1)
    sums = Total(1, jnp.concatenate([tile, jnp.zeros_like(tile)], axis=0))

    apply(dir1, img1, weighted_cells, (sums.advance,) * 3)
    next_norm = sums.read(0)
    beta = next_norm / norm
    dir1[...] = dir1[...] + beta[None] * dir0[...]
    tile = tile_of(dir1[...] * img1[...]) + beta * own_tile(dir1, img0)
    sums = Total(2, jnp.concatenate([tile, jnp.zeros_like(tile)], axis=0))
    exchange(((img1, 4),), (sums.advance,) * 3)
    second_step = next_norm / sums.read(0)
    for t in range(time_n):
        at = (t + 2, own_a)
        step = first_step * dir0[at] + second_step * dir1[at]
        left = res[at] - second_step * (img1[at] + beta * img0[at])
        step_ref[t] = step[:, 0:lon_n]
        resid_ref[t] = left[:, 0:lon_n]
    for condition, copy in pending:
        if condition is None:
            copy.wait_send()
        else:
            pl.when(condition)(copy.wait_send)


def solution(mesh):
    mesh_sizes = tuple(mesh.shape[name] for name in AXES)

    def per_device(precip, offset, coefficients, inverse_diag):
        time_n, lat_n, lon_n = coefficients.shape
        hours, lat_cells, lon_cells = precip.shape
        assert lon_cells == LANES and 3 * (lon_n + 8) <= LANES and 8 * (time_n + 4) <= LANES
        rows = lat_n + 2 * LEAD
        padded_time = time_n + 4
        lat_fwd, lat_back = lat_tables(lat_n)
        lon_fwd, lon_high, lon_low = lon_tables(lon_n)
        knots = pltpu.VMEM((padded_time, rows, LANES), f32)
        n_lon, n_lat, n_tm = mesh_sizes
        banks, totals = 5, 3
        vmem = pl.BlockSpec(memory_space=pltpu.VMEM)
        hbm = pl.BlockSpec(memory_space=pl.ANY)
        shape = jax.ShapeDtypeStruct(coefficients.shape, f32)
        dma = pltpu.SemaphoreType.DMA
        return pl.pallas_call(
            functools.partial(kernel, (time_n, lat_n, lon_n), mesh_sizes),
            out_shape=(shape, shape),
            in_specs=[vmem, vmem, hbm, hbm, hbm] + [vmem] * 5,
            out_specs=(vmem, vmem),
            scratch_shapes=[
                pltpu.VMEM((hours, lat_cells, lon_cells), f32),
                pltpu.VMEM((hours, lat_cells, lon_cells), f32),
                pltpu.VMEM((lat_cells, LANES), f32),
                pltpu.VMEM((lat_cells, padded_time * LANES), f32),
            ]
            + [knots] * 7
            + [
                pltpu.VMEM((banks, LANES, LANES), f32),
                pltpu.VMEM((banks, LANES, LANES), f32),
                pltpu.VMEM((banks, 2, 4 * padded_time, LANES), f32),
                pltpu.VMEM((banks, 2, 4 * padded_time, LANES), f32),
                pltpu.VMEM((banks, 2, 2, rows, LANES), f32),
                pltpu.VMEM((banks, 2, 2, rows, LANES), f32),
                pltpu.VMEM((totals, n_lon, 16, LANES), f32),
                pltpu.VMEM((totals, n_lat, 16, LANES), f32),
                pltpu.VMEM((totals, n_tm, 16, LANES), f32),
                dma((5,)),
                dma((2, 2 * banks)),
                dma((2, 2 * banks)),
                dma((2, 2 * banks)),
                dma((2, totals * n_lon)),
                dma((2, totals * n_lat)),
                dma((2, totals * n_tm)),
            ],
            compiler_params=pltpu.CompilerParams(
                collective_id=0, has_side_effects=True, vmem_limit_bytes=60 * 1024 * 1024
            ),
        )(
            coefficients,
            inverse_diag,
            jnp.asarray(area_table(lat_cells * n_lat)),
            offset,
            precip,
            jnp.asarray(lon_fwd),
            jnp.asarray(lat_fwd),
            jnp.asarray(lat_back),
            jnp.asarray(lon_high),
            jnp.asarray(lon_low),
        )

    spec = P("tm", "lat", "lon")
    return jax.shard_map(
        per_device,
        mesh=mesh,
        in_specs=(spec,) * 4,
        out_specs=(spec,) * 2,
        check_vma=False,
    )
```

time: 330 us -> 74.3 us (0.23); the launches traced: 324 us -> 74.1 us
  blocking collectives: 116 us -> 0 us
  starting transfers between devices: 80 us -> 0 us
  waiting for transfers between devices: 67.6 us -> 0 us
  Pallas kernels: 0 us -> 66.5 us
  matrix products: 43.5 us -> 0 us
  other arithmetic: 8.67 us -> 0 us
  between operations: 5.66 us -> 0.64 us
  local copies, waits for them, and re-layouts: 2.82 us -> 6.92 us
    psum x3 -> x0, blocking collectives: 116 us -> none  [global_sum(): return lax.psum(values, ('lon', 'lat', 'tm'))]
    ppermute x36 -> x0, starting transfers between devices: 80 us -> none  [the longest x18 56.7 us: with_halo(): lax.ppermute(tail, axis, [(i, (i + 1) % count) for i in range(ends)])]
    ppermute x36 -> x0, waiting for transfers between devices: 67.6 us -> none  [the longest x18 49.2 us: with_halo(): lax.ppermute(head, axis, [((i + 1) % count, i) for i in range(ends)])]
    pallas_call x0 -> x1, Pallas kernels: none -> 66.5 us  [per_device(): pl.pallas_call(functools.partial(kernel, (time_n, lat_n, lon_n), mesh_siz...]
    dot_general x18 -> x0, matrix products: 43.5 us -> none  [the longest x3 14.9 us: evaluate(): return jnp.einsum('tbl,st->sbl', partial_value, time_tab, precision=highest)]
    pallas_call x0 -> x2, local copies, waits for them, and re-layouts: none -> 3.46 us  [per_device(): pl.pallas_call(functools.partial(kernel, (time_n, lat_n, lon_n), mesh_siz...]
  transfers between devices with their start and end apart: 36 -> 0, of which waited for: 29 -> 0; matrix products, arithmetic and copies ran while one was open for 1% -> 0% of each run, Pallas kernels for 0% -> 0%
where the time goes in v1:
time: 74.3 us; the launch traced here: 74.1 us
  Pallas kernels  66.5 us (90%)
  local copies, waits for them, and re-layouts  6.92 us (9%)
    pallas_call x1, Pallas kernels, per_device(): pl.pallas_call(functools.partial(kernel, (time_n, lat_n, lon_n), mesh_siz...  66.5 us
    unnamed x2, local copies, waits for them, and re-layouts  3.46 us
    pallas_call x2, local copies, waits for them, and re-layouts, per_device(): pl.pallas_call(functools.partial(kernel, (time_n, lat_n, lon_n), mesh_siz...  3.46 us

profile of v1, /device:TPU:1, one launch (start us, length us, event | category | flops | bytes accessed | tf_op | source)
XLA Modules:
  0.0 74.1 jit_solution(7480721037020149329)
XLA Ops:
  0.6 1.7 %copy.12.coef_ref = f32[8,64,32]{2,1,0:T(8,128)} copy(f32[8,64,32]{1,2,0:T(8,128)} %param.12) | data formatting | bytes 131072 | tf_op args[2]
  2.4 1.7 %copy.13.inv_ref = f32[8,64,32]{2,1,0:T(8,128)} copy(f32[8,64,32]{1,2,0:T(8,128)} %param.13) | data formatting | bytes 131072 | tf_op args[3]
  4.1 66.5 %shard_map.113 = (f32[8,64,32]{2,1,0:T(8,128)}, f32[8,64,32]{2,1,0:T(8,128)}) custom-call(f32[8,64,32]{2,1,0:T(8,128)} %copy.12.coef_ref, f32[8,64,32]{2,1,0:T(8,128)} %copy.13.inv_ref, f32[1024,128]{1,0:T(8,128)} %constant.12.clone.area_hbm, f32[32,256,128]{2,1,0:T(8,128)} %offset_hbm.1, f32[32,256,128]{2,1,0:T(8,128)} %precip_hbm.1, ...), custom_call_target="tpu_custom_call" | custom-call | tf_op jit(solution)/shard_map/pallas_call | solution.py:484
  70.6 1.7 %copy.14 = f32[8,64,32]{1,2,0:T(8,128)} copy(f32[8,64,32]{2,1,0:T(8,128)} %get-tuple-element.2) | data formatting | bytes 131072 | tf_op jit(solution)/shard_map/pallas_call | solution.py:484
  72.3 1.7 %copy.15 = f32[8,64,32]{1,2,0:T(8,128)} copy(f32[8,64,32]{2,1,0:T(8,128)} %get-tuple-element.3) | data formatting | bytes 131072 | tf_op jit(solution)/shard_map/pallas_call | solution.py:484

commit v2 on v1

--- a/solution.py
+++ b/solution.py
@@ -160,15 +160,23 @@
 
     coef[...] = jnp.zeros(coef.shape, f32)
     inv[...] = jnp.zeros(inv.shape, f32)
-    coef[own_t, own_a, 0:lon_n] = coef_ref[...]
-    inv[own_t, own_a, 0:lon_n] = inv_ref[...]
-    pl.semaphore_wait(barrier, sum(size[name] - 1 for name in AXES))
-
     lane = lax.broadcasted_iota(jnp.int32, (rows, LANES), 1)
     low_lanes = (lane < 2) | (lane >= LANES - 2)
     high_lanes = (lane >= lon_n - 2) & (lane < lon_n + 2)
     used_lanes = (lane < lon_n + 2) | (lane >= LANES - 2)
     own_lanes = lane[0:lat_n] < lon_n
+    batch = LANES // lon_n
+
+    for source, held in ((coef_ref, coef), (inv_ref, inv)):
+        for first in range(0, time_n, batch):
+            block = source[first : first + batch].reshape(LANES, lat_n)
+            if lat_n < LANES:
+                block = jnp.concatenate([block, jnp.zeros((LANES, LANES - lat_n), f32)], axis=1)
+            turned = block.T[0:lat_n]
+            for i in range(batch):
+                slab = pltpu.roll(turned, LANES - lon_n * i, 1) if i else turned
+                held[2 + first + i, own_a] = jnp.where(own_lanes, slab, 0.0)
+    pl.semaphore_wait(barrier, sum(size[name] - 1 for name in AXES))
 
     def remote(src, dst, sems, at, name, to):
         return pltpu.make_async_remote_copy(
@@ -450,12 +458,20 @@
     sums = Total(2, jnp.concatenate([tile, jnp.zeros_like(tile)], axis=0))
     exchange(((img1, 4),), (sums.advance,) * 3)
     second_step = next_norm / sums.read(0)
-    for t in range(time_n):
-        at = (t + 2, own_a)
-        step = first_step * dir0[at] + second_step * dir1[at]
-        left = res[at] - second_step * (img1[at] + beta * img0[at])
-        step_ref[t] = step[:, 0:lon_n]
-        resid_ref[t] = left[:, 0:lon_n]
+    for first in range(0, time_n, batch):
+        packed = [None, None]
+        for i in range(batch):
+            at = (first + i + 2, own_a)
+            step = first_step * dir0[at] + second_step * dir1[at]
+            left = res[at] - second_step * (img1[at] + beta * img0[at])
+            for which, value in enumerate((step, left)):
+                slab = jnp.where(own_lanes, value, 0.0)
+                slab = pltpu.roll(slab, lon_n * i, 1) if i else slab
+                packed[which] = slab if i == 0 else packed[which] + slab
+        for ref, value in zip((step_ref, resid_ref), packed):
+            if lat_n < LANES:
+                value = jnp.concatenate([value, jnp.zeros((LANES - lat_n, LANES), f32)], axis=0)
+            ref[first : first + batch] = value.T[:, 0:lat_n].reshape(batch, lon_n, lat_n)
     for condition, copy in pending:
         if condition is None:
             copy.wait_send()
@@ -470,6 +486,7 @@
         time_n, lat_n, lon_n = coefficients.shape
         hours, lat_cells, lon_cells = precip.shape
         assert lon_cells == LANES and 3 * (lon_n + 8) <= LANES and 8 * (time_n + 4) <= LANES
+        assert LANES % lon_n == 0 and time_n % (LANES // lon_n) == 0 and lat_n <= LANES
         rows = lat_n + 2 * LEAD
         padded_time = time_n + 4
         lat_fwd, lat_back = lat_tables(lat_n)
@@ -479,9 +496,9 @@
         banks, totals = 5, 3
         vmem = pl.BlockSpec(memory_space=pltpu.VMEM)
         hbm = pl.BlockSpec(memory_space=pl.ANY)
-        shape = jax.ShapeDtypeStruct(coefficients.shape, f32)
+        shape = jax.ShapeDtypeStruct((time_n, lon_n, lat_n), f32)
         dma = pltpu.SemaphoreType.DMA
-        return pl.pallas_call(
+        step, left = pl.pallas_call(
             functools.partial(kernel, (time_n, lat_n, lon_n), mesh_sizes),
             out_shape=(shape, shape),
             in_specs=[vmem, vmem, hbm, hbm, hbm] + [vmem] * 5,
@@ -515,8 +532,8 @@
                 collective_id=0, has_side_effects=True, vmem_limit_bytes=60 * 1024 * 1024
             ),
         )(
-            coefficients,
-            inverse_diag,
+            jnp.swapaxes(coefficients, 1, 2),
+            jnp.swapaxes(inverse_diag, 1, 2),
             jnp.asarray(area_table(lat_cells * n_lat)),
             offset,
             precip,
@@ -526,6 +543,7 @@
             jnp.asarray(lon_high),
             jnp.asarray(lon_low),
         )
+        return jnp.swapaxes(step, 1, 2), jnp.swapaxes(left, 1, 2)
 
     spec = P("tm", "lat", "lon")
     return jax.shard_map(

time: 74.3 us -> 70.5 us (0.949)
  local copies, waits for them, and re-layouts: 6.92 us -> 3.14 us
    pallas_call x2 -> x0, local copies, waits for them, and re-layouts: 3.46 us -> none  [per_device(): pl.pallas_call(functools.partial(kernel, (time_n, lat_n, lon_n), mesh_siz...]
where the time goes in v2:
time: 70.5 us; the launch traced here: 70.4 us
  Pallas kernels  66.6 us (94%)
  local copies, waits for them, and re-layouts  3.14 us (4%)
    pallas_call x1, Pallas kernels, per_device(): pl.pallas_call(functools.partial(kernel, (time_n, lat_n, lon_n), mesh_siz...  66.6 us
    unnamed x2, local copies, waits for them, and re-layouts  3.14 us

profile of v2, /device:TPU:1, one launch (start us, length us, event | category | flops | bytes accessed | tf_op | source)
XLA Modules:
  0.0 70.4 jit_solution(1849388739841520611)
XLA Ops:
  0.6 66.6 %shard_map.113 = (f32[8,32,64]{2,1,0:T(8,128)}, f32[8,32,64]{2,1,0:T(8,128)}) custom-call(f32[8,32,64]{2,1,0:T(8,128)} %bitcast.4, f32[8,32,64]{2,1,0:T(8,128)} %bitcast.5, f32[1024,128]{1,0:T(8,128)} %constant.12.clone.area_hbm, f32[32,256,128]{2,1,0:T(8,128)} %offset_hbm.1, f32[32,256,128]{2,1,0:T(8,128)} %precip_hbm.1, ...), custom_call_target="tpu_custom_call" | custom-call | tf_op jit(solution)/shard_map/pallas_call | solution.py:501
  67.2 1.6 %copy.14 = f32[8,64,32]{1,2,0:T(8,128)} copy(f32[8,64,32]{1,2,0:T(8,128)} %bitcast.7) | data formatting | bytes 131072
  68.8 1.6 %copy.15 = f32[8,64,32]{1,2,0:T(8,128)} copy(f32[8,64,32]{1,2,0:T(8,128)} %bitcast.6) | data formatting | bytes 131072

commit v3 on v2

--- a/solution.py
+++ b/solution.py
@@ -109,6 +109,7 @@
     lon_recv,
     lat_send,
     lat_recv,
+    diag_recv,
     tm_send,
     tm_recv,
     sum_lon,
@@ -117,6 +118,7 @@
     load_sem,
     lon_sems,
     lat_sems,
+    diag_sems,
     tm_sems,
     sum_lon_sems,
     sum_lat_sems,
@@ -157,6 +159,17 @@
                 device_id={name: lax.rem(me[name] + hop, size[name])},
                 device_id_type=pl.DeviceIdType.MESH,
             )
+    for hop in (1, size["lon"] - 1):
+        for rise in (1, size["lat"] - 1):
+            pl.semaphore_signal(
+                barrier,
+                inc=1,
+                device_id={
+                    "lon": lax.rem(me["lon"] + hop, size["lon"]),
+                    "lat": lax.rem(me["lat"] + rise, size["lat"]),
+                },
+                device_id_type=pl.DeviceIdType.MESH,
+            )
 
     coef[...] = jnp.zeros(coef.shape, f32)
     inv[...] = jnp.zeros(inv.shape, f32)
@@ -165,6 +178,7 @@
     high_lanes = (lane >= lon_n - 2) & (lane < lon_n + 2)
     used_lanes = (lane < lon_n + 2) | (lane >= LANES - 2)
     own_lanes = lane[0:lat_n] < lon_n
+    strip = lax.broadcasted_iota(jnp.int32, (4 * padded_time, LANES), 1)
     batch = LANES // lon_n
 
     for source, held in ((coef_ref, coef), (inv_ref, inv)):
@@ -176,7 +190,7 @@
             for i in range(batch):
                 slab = pltpu.roll(turned, LANES - lon_n * i, 1) if i else turned
                 held[2 + first + i, own_a] = jnp.where(own_lanes, slab, 0.0)
-    pl.semaphore_wait(barrier, sum(size[name] - 1 for name in AXES))
+    pl.semaphore_wait(barrier, 4 + sum(size[name] - 1 for name in AXES))
 
     def remote(src, dst, sems, at, name, to):
         return pltpu.make_async_remote_copy(
@@ -184,7 +198,7 @@
             dst_ref=dst,
             send_sem=sems.at[0, at],
             recv_sem=sems.at[1, at],
-            device_id={name: to},
+            device_id=to if isinstance(to, dict) else {name: to},
             device_id_type=pl.DeviceIdType.MESH,
         )
 
@@ -194,7 +208,54 @@
 
     def exchange(pairs, hooks):
         copies = []
+        corners = []
+        has_lat = (me["lat"] > 0, me["lat"] < size["lat"] - 1)
         before, after = neighbours("lon")
+
+        def ends(name, send, recv, sems, load, store):
+            before, after = neighbours(name)
+            has_low = me[name] > 0
+            has_high = me[name] < size[name] - 1
+            copies = []
+            for ref, bank in pairs:
+                load(ref, bank)
+                down = remote(send.at[bank, 0], recv.at[bank, 1], sems, 2 * bank, name, before)
+                up = remote(send.at[bank, 1], recv.at[bank, 0], sems, 2 * bank + 1, name, after)
+                pl.when(has_low)(down.start)
+                pl.when(has_high)(up.start)
+                copies.append((down, up))
+                pending.append((has_low, down))
+                pending.append((has_high, up))
+
+            def finish():
+                for (ref, bank), (down, up) in zip(pairs, copies):
+
+                    @pl.when(has_low)
+                    def _():
+                        up.wait_recv()
+                        store(ref, bank, 0)
+
+                    @pl.when(has_high)
+                    def _():
+                        down.wait_recv()
+                        store(ref, bank, 1)
+
+            return finish
+
+        starts = (LEAD - 2, LEAD + lat_n - 2)
+
+        def lat_load(ref, bank):
+            for t in range(padded_time):
+                for side, start in enumerate(starts):
+                    lat_send[bank, side, 4 * t : 4 * t + 4] = ref[t, start : start + 4]
+
+        def lat_store(ref, bank, side):
+            start = starts[side]
+            for t in range(padded_time):
+                ref[t, start : start + 4] = (
+                    ref[t, start : start + 4] + lat_recv[bank, side, 4 * t : 4 * t + 4]
+                )
+
         for ref, bank in pairs:
             packed = jnp.zeros((rows, LANES), f32)
             for t in range(padded_time):
@@ -224,10 +285,39 @@
             copies.append((down, up))
             pending.append((None, down))
             pending.append((None, up))
+            lats = neighbours("lat")
+            corner = {}
+            for side, (span, to) in enumerate(((low, before), (high, after))):
+                for rise in range(2):
+                    copy = remote(
+                        lon_send.at[bank, span],
+                        diag_recv.at[bank, 1 - side, 1 - rise],
+                        diag_sems,
+                        4 * bank + 2 * side + rise,
+                        "lat",
+                        {"lon": to, "lat": lats[rise]},
+                    )
+                    pl.when(has_lat[rise])(copy.start)
+                    pending.append((has_lat[rise], copy))
+                    corner[1 - side, 1 - rise] = copy
+            corners.append(corner)
+        finish_lat = ends("lat", lat_send, lat_recv, lat_sems, lat_load, lat_store)
         hooks[0]()
-        for (ref, bank), (down, up) in zip(pairs, copies):
+        for (ref, bank), (down, up), corner in zip(pairs, copies, corners):
             down.wait_recv()
             up.wait_recv()
+            for rise in range(2):
+
+                @pl.when(has_lat[rise])
+                def _():
+                    start = LEAD - 2 + rise * lat_n
+                    turn = lat_n if rise else LANES - lat_n
+                    for side, span in enumerate((low, high)):
+                        corner[side, rise].wait_recv()
+                        got = pltpu.roll(diag_recv[bank, side, rise], turn % LANES, 1)
+                        got = jnp.where((strip >= start) & (strip < start + 4), got, 0.0)
+                        lon_recv[bank, span] = lon_recv[bank, span] + got
+
             back = lon_recv[bank].T[0:rows]
             for t in range(padded_time):
                 at = 4 * t
@@ -236,48 +326,7 @@
                 mine = jnp.where(high_lanes, pltpu.roll(back, (LANES - at + lon_n - 2) % LANES, 1), mine)
                 ref[t] = ref[t] + mine
 
-        def ends(name, send, recv, sems, load, store, hook):
-            before, after = neighbours(name)
-            has_low = me[name] > 0
-            has_high = me[name] < size[name] - 1
-            copies = []
-            for ref, bank in pairs:
-                load(ref, bank)
-                down = remote(send.at[bank, 0], recv.at[bank, 1], sems, 2 * bank, name, before)
-                up = remote(send.at[bank, 1], recv.at[bank, 0], sems, 2 * bank + 1, name, after)
-                pl.when(has_low)(down.start)
-                pl.when(has_high)(up.start)
-                copies.append((down, up))
-                pending.append((has_low, down))
-                pending.append((has_high, up))
-            hook()
-            for (ref, bank), (down, up) in zip(pairs, copies):
-
-                @pl.when(has_low)
-                def _():
-                    up.wait_recv()
-                    store(ref, bank, 0)
-
-                @pl.when(has_high)
-                def _():
-                    down.wait_recv()
-                    store(ref, bank, 1)
-
-        starts = (LEAD - 2, LEAD + lat_n - 2)
-
-        def lat_load(ref, bank):
-            for t in range(padded_time):
-                for side, start in enumerate(starts):
-                    lat_send[bank, side, 4 * t : 4 * t + 4] = ref[t, start : start + 4]
-
-        def lat_store(ref, bank, side):
-            start = starts[side]
-            for t in range(padded_time):
-                ref[t, start : start + 4] = (
-                    ref[t, start : start + 4] + lat_recv[bank, side, 4 * t : 4 * t + 4]
-                )
-
-        ends("lat", lat_send, lat_recv, lat_sems, lat_load, lat_store, hooks[1])
+        finish_lat()
 
         def tm_load(ref, bank):
             for side, start in enumerate((0, time_n)):
@@ -295,7 +344,10 @@
                     used_lanes, pltpu.roll(got, half, 1), 0.0
                 )
 
-        ends("tm", tm_send, tm_recv, tm_sems, tm_load, tm_store, hooks[2])
+        finish_tm = ends("tm", tm_send, tm_recv, tm_sems, tm_load, tm_store)
+        hooks[1]()
+        finish_tm()
+        hooks[2]()
 
     slots = {"lon": sum_lon, "lat": sum_lat, "tm": sum_tm}
     slot_sems = {"lon": sum_lon_sems, "lat": sum_lat_sems, "tm": sum_tm_sems}
@@ -477,6 +529,11 @@
             copy.wait_send()
         else:
             pl.when(condition)(copy.wait_send)
+
+
+def hand_on(step_ref, resid_ref, step_out, resid_out):
+    step_out[...] = step_ref[...]
+    resid_out[...] = resid_ref[...]
 
 
 def solution(mesh):
@@ -515,6 +572,7 @@
                 pltpu.VMEM((banks, LANES, LANES), f32),
                 pltpu.VMEM((banks, 2, 4 * padded_time, LANES), f32),
                 pltpu.VMEM((banks, 2, 4 * padded_time, LANES), f32),
+                pltpu.VMEM((banks, 2, 2, 4 * padded_time, LANES), f32),
                 pltpu.VMEM((banks, 2, 2, rows, LANES), f32),
                 pltpu.VMEM((banks, 2, 2, rows, LANES), f32),
                 pltpu.VMEM((totals, n_lon, 16, LANES), f32),
@@ -523,6 +581,7 @@
                 dma((5,)),
                 dma((2, 2 * banks)),
                 dma((2, 2 * banks)),
+                dma((2, 4 * banks)),
                 dma((2, 2 * banks)),
                 dma((2, totals * n_lon)),
                 dma((2, totals * n_lat)),
@@ -543,6 +602,9 @@
             jnp.asarray(lon_high),
             jnp.asarray(lon_low),
         )
+        step, left = pl.pallas_call(
+            hand_on, out_shape=(shape, shape), in_specs=[vmem, vmem], out_specs=(vmem, vmem)
+        )(step, left)
         return jnp.swapaxes(step, 1, 2), jnp.swapaxes(left, 1, 2)
 
     spec = P("tm", "lat", "lon")

time: 70.5 us -> 69.3 us (0.983)
  local copies, waits for them, and re-layouts: 3.14 us -> 0 us
  Pallas kernels: 66.6 us -> 68.1 us
    unnamed x2 -> x0, local copies, waits for them, and re-layouts: 3.14 us -> none
    pallas_call x0 -> x1, Pallas kernels: none -> 1.68 us  [per_device(): pl.pallas_call(hand_on, out_shape=(shape, shape), in_specs=[vmem, vmem],...]
where the time goes in v3:
time: 69.3 us; the launch traced here: 68.8 us
  Pallas kernels  68.1 us (98%)
    pallas_call x1, Pallas kernels, per_device(): pl.pallas_call(functools.partial(kernel, (time_n, lat_n, lon_n), mesh_siz...  66.5 us
    pallas_call x1, Pallas kernels, per_device(): pl.pallas_call(hand_on, out_shape=(shape, shape), in_specs=[vmem, vmem],...  1.68 us

profile of v3, /device:TPU:1, one launch (start us, length us, event | category | flops | bytes accessed | tf_op | source)
XLA Modules:
  0.0 68.8 jit_solution(18392465274739485520)
XLA Ops:
  0.6 66.5 %shard_map.113 = (f32[8,32,64]{2,1,0:T(8,128)}, f32[8,32,64]{2,1,0:T(8,128)}) custom-call(f32[8,32,64]{2,1,0:T(8,128)} %bitcast.4, f32[8,32,64]{2,1,0:T(8,128)} %bitcast.5, f32[1024,128]{1,0:T(8,128)} %constant.12.clone.area_hbm, f32[32,256,128]{2,1,0:T(8,128)} %offset_hbm.1, f32[32,256,128]{2,1,0:T(8,128)} %precip_hbm.1, ...), custom_call_target="tpu_custom_call" | custom-call | tf_op jit(solution)/shard_map/pallas_call | solution.py:558
  67.1 1.7 %shard_map.114 = (f32[8,32,64]{2,1,0:T(8,128)}, f32[8,32,64]{2,1,0:T(8,128)}) custom-call(f32[8,32,64]{2,1,0:T(8,128)} %get-tuple-element.6.step_ref, f32[8,32,64]{2,1,0:T(8,128)} %get-tuple-element.7.resid_ref), custom_call_target="tpu_custom_call" | custom-call | tf_op jit(solution)/shard_map/pallas_call | solution.py:605

commit v4 on v2

--- a/solution.py
+++ b/solution.py
@@ -33,7 +33,9 @@
 def lat_tables(count):
     knots = np.arange(count + 2 * LEAD) - LEAD
     cells = np.arange(4 * count)
-    high, low = halves(spline((cells[:, None] - 4.0 * knots[None, :] - 1.5) / 4.0))
+    high, low = halves(
+        float(spline(0.125)) * spline((cells[:, None] - 4.0 * knots[None, :] - 1.5) / 4.0)
+    )
     forward = np.concatenate([high, high, low], axis=1)
     back = np.concatenate([high.T, low.T], axis=0)
     return forward, back
@@ -67,7 +69,7 @@
     for phase in range(4):
         row = []
         for shift in range(-2, 3):
-            weight = float(spline((phase - 4.0 * shift - 1.5) / 4.0))
+            weight = float(spline((phase - 4.0 * shift - 1.5) / 4.0) / spline(0.125))
             if weight != 0.0:
                 row.append((shift + 2, weight))
         taps.append(row)
@@ -350,7 +352,7 @@
     def synth(z, m, phase):
         total = None
         for at, factor in taps[phase]:
-            term = z[m + at] * factor
+            term = z[m + at] if factor == 1.0 else z[m + at] * factor
             total = term if total is None else total + term
         return total
 
@@ -377,12 +379,15 @@
             z = [cells[at, columns(t)] for t in range(padded_time)]
             sums = [None] * padded_time
             for m in range(time_n):
+                values = [cell_values(4 * m + phase, at, synth(z, m, phase)) for phase in range(4)]
+                terms = [(2, values[1] + values[2]), (2, (values[0] + values[3]) * dict(taps[0])[2])]
                 for phase in range(4):
-                    value = cell_values(4 * m + phase, at, synth(z, m, phase))
                     for shift, factor in taps[phase]:
-                        term = value * factor
-                        old = sums[m + shift]
-                        sums[m + shift] = term if old is None else old + term
+                        if shift != 2:
+                            terms.append((shift, values[phase] * factor))
+                for shift, term in terms:
+                    old = sums[m + shift]
+                    sums[m + shift] = term if old is None else old + term
                 cells[at, columns(m)] = sums[m]
             for t in range(time_n, padded_time):
                 cells[at, columns(t)] = sums[t]
@@ -477,6 +482,11 @@
             copy.wait_send()
         else:
             pl.when(condition)(copy.wait_send)
+
+
+def hand_on(step_ref, resid_ref, step_out, resid_out):
+    step_out[...] = step_ref[...]
+    resid_out[...] = resid_ref[...]
 
 
 def solution(mesh):
@@ -543,6 +553,9 @@
             jnp.asarray(lon_high),
             jnp.asarray(lon_low),
         )
+        step, left = pl.pallas_call(
+            hand_on, out_shape=(shape, shape), in_specs=[vmem, vmem], out_specs=(vmem, vmem)
+        )(step, left)
         return jnp.swapaxes(step, 1, 2), jnp.swapaxes(left, 1, 2)
 
     spec = P("tm", "lat", "lon")

time: 70.5 us -> 68.7 us (0.974)
  local copies, waits for them, and re-layouts: 3.14 us -> 0 us
  Pallas kernels: 66.6 us -> 67.9 us
    unnamed x2 -> x0, local copies, waits for them, and re-layouts: 3.14 us -> none
    pallas_call x0 -> x1, Pallas kernels: none -> 1.68 us  [per_device(): pl.pallas_call(hand_on, out_shape=(shape, shape), in_specs=[vmem, vmem],...]
where the time goes in v4:
time: 68.7 us; the launch traced here: 68.6 us
  Pallas kernels  67.9 us (99%)
    pallas_call x1, Pallas kernels, per_device(): pl.pallas_call(functools.partial(kernel, (time_n, lat_n, lon_n), mesh_siz...  66.3 us
    pallas_call x1, Pallas kernels, per_device(): pl.pallas_call(hand_on, out_shape=(shape, shape), in_specs=[vmem, vmem],...  1.68 us

profile of v4, /device:TPU:1, one launch (start us, length us, event | category | flops | bytes accessed | tf_op | source)
XLA Modules:
  0.0 68.6 jit_solution(17980979734415365643)
XLA Ops:
  0.6 66.3 %shard_map.113 = (f32[8,32,64]{2,1,0:T(8,128)}, f32[8,32,64]{2,1,0:T(8,128)}) custom-call(f32[8,32,64]{2,1,0:T(8,128)} %bitcast.4, f32[8,32,64]{2,1,0:T(8,128)} %bitcast.5, f32[1024,128]{1,0:T(8,128)} %constant.12.clone.area_hbm, f32[32,256,128]{2,1,0:T(8,128)} %offset_hbm.1, f32[32,256,128]{2,1,0:T(8,128)} %precip_hbm.1, ...), custom_call_target="tpu_custom_call" | custom-call | tf_op jit(solution)/shard_map/pallas_call | solution.py:511
  66.9 1.7 %shard_map.114 = (f32[8,32,64]{2,1,0:T(8,128)}, f32[8,32,64]{2,1,0:T(8,128)}) custom-call(f32[8,32,64]{2,1,0:T(8,128)} %get-tuple-element.6.step_ref, f32[8,32,64]{2,1,0:T(8,128)} %get-tuple-element.7.resid_ref), custom_call_target="tpu_custom_call" | custom-call | tf_op jit(solution)/shard_map/pallas_call | solution.py:556
